TPU v7x, 128 devices: a whole 4x4x4 slice. The times are simulated.
128 devices in a mesh: dp: 16 (over x, z_lo, core), graph: 8 (over z_hi, y).
Axes of the slice: x: 4, y: 4, z: 4 (z_hi: 2, z_lo: 2; z = z_hi * 2 + z_lo), core: 2. Of those that a mesh axis runs over, the one named last changes fastest.
Arguments:
- nodes: bfloat16 [16, 128, 6272], P('dp', 'graph'), may hold values from -6 to 6
- sources: int32 [16, 4096], P('dp', 'graph'), may hold values from 0 to 127
- targets: int32 [16, 4096], P('dp', 'graph'), may hold values from 0 to 127
- edge_counts: int32 [16, 8], P('dp', 'graph'), may hold values from 128 to 512, as said below
- wigner: bfloat16 [16, 29, 49, 4096], P('dp', None, None, 'graph'), as said below
- radial: bfloat16 [16, 4096, 128], P('dp', 'graph'), may hold values from 0.5 to 1.5
- cotangent: bfloat16 [16, 128, 6272], P('dp', 'graph'), may hold values from -6 to 6
- w_zero: bfloat16 [896, 896], replicated, may hold values from -0.1875 to 0.1875
- w_one: bfloat16 [2, 768, 768], replicated, may hold values from -0.15625 to 0.15625
- w_two: bfloat16 [2, 640, 640], replicated, may hold values from -0.15625 to 0.15625
- w_gate: bfloat16 [128, 128], replicated, may hold values from -0.5 to 0.5
Outputs:
- aggregated: bfloat16 [16, 128, 6272], P('dp', 'graph')
- grad_nodes: bfloat16 [16, 128, 6272], P('dp', 'graph')
- grad_zero: float32 [896, 896], replicated
- grad_one: float32 [2, 768, 768], replicated
- grad_two: float32 [2, 640, 640], replicated
- grad_gate: float32 [128, 128], replicated
Inputs may be any that keep to these rules, and one draw needn't show every extreme that they name: `edge_counts`: one shard of each batch holds 512 live slots; live slots come first in each shard. `wigner`: for each edge, entry (k, j) is zero unless kept coefficient k and coefficient j have the same degree.
All inputs are finite; a program needn't handle non-finite values.
Results may differ from a plain program's by a relative error of at most 0.013.
Values may be sent and summed in bfloat16 or wider, within the bound.
A program may use at most 128 MiB of HBM per device.

v0:
```python
import jax
import jax.numpy as jnp
from jax import lax
from jax.sharding import PartitionSpec as P


def product(left, right):
    return jnp.dot(left, right, preferred_element_type=jnp.float32)


def product_left(left, right):
    return lax.dot_general(
        left, right, (((0,), (0,)), ((), ())), preferred_element_type=jnp.float32
    )


def product_right(left, right):
    return lax.dot_general(
        left, right, (((1,), (1,)), ((), ())), preferred_element_type=jnp.float32
    )


def split_kept(values):
    rows = values.shape[0]
    bounds = ((0, 7), (7, 13), (13, 19), (19, 24), (24, 29))
    return tuple((values[:, lower:upper, :].reshape(rows, -1) for lower, upper in bounds))


def edge_forward(gathered, rotation, radial_rows, valid, w_zero, w_one, w_two, w_gate):
    rows = gathered.shape[0]
    width = w_gate.shape[0]
    turned = jnp.einsum("kje,ejc->ekc", rotation, gathered, preferred_element_type=jnp.float32)
    rotated = (turned * radial_rows.astype(jnp.float32)[:, None, :]).astype(jnp.bfloat16)
    zero_part, plus_one, minus_one, plus_two, minus_two = split_kept(rotated)
    mixed = jnp.concatenate(
        [
            product(zero_part, w_zero),
            product(plus_one, w_one[0]) - product(minus_one, w_one[1]),
            product(plus_one, w_one[1]) + product(minus_one, w_one[0]),
            product(plus_two, w_two[0]) - product(minus_two, w_two[1]),
            product(plus_two, w_two[1]) + product(minus_two, w_two[0]),
        ],
        axis=1,
    ).reshape(rows, -1, width)
    scalar = mixed[:, 0, :]
    scalar_low = scalar.astype(jnp.bfloat16)
    gate = jax.nn.sigmoid(product(scalar_low, w_gate))
    message = jnp.concatenate(
        [jax.nn.silu(scalar)[:, None, :], mixed[:, 1:, :] * gate[:, None, :]], axis=1
    )
    message = (message * valid[:, None, None].astype(jnp.float32)).astype(jnp.bfloat16)
    back = jnp.einsum("kje,ekc->ejc", rotation, message, preferred_element_type=jnp.float32).astype(
        jnp.bfloat16
    )
    return (back, (rotated, mixed, scalar_low, gate))


def edge_backward(upstream, rotation, radial_rows, saved, w_zero, w_one, w_two, w_gate):
    rotated, mixed, scalar_low, gate = saved
    rows = upstream.shape[0]
    width = w_gate.shape[0]
    incoming = jnp.einsum("kje,ejc->ekc", rotation, upstream, preferred_element_type=jnp.float32)
    scalar = mixed[:, 0, :]
    sigmoid_value = jax.nn.sigmoid(scalar)
    direct = incoming[:, 0, :] * sigmoid_value * (1.0 + scalar * (1.0 - sigmoid_value))
    gate_low = (jnp.sum(incoming[:, 1:, :] * mixed[:, 1:, :], axis=1) * gate * (1.0 - gate)).astype(
        jnp.bfloat16
    )
    head = direct + product_right(gate_low, w_gate)
    mixed_grad = jnp.concatenate(
        [head[:, None, :], incoming[:, 1:, :] * gate[:, None, :]], axis=1
    ).astype(jnp.bfloat16)
    zero_grad, plus_one_grad, minus_one_grad, plus_two_grad, minus_two_grad = split_kept(mixed_grad)
    zero_part, plus_one, minus_one, plus_two, minus_two = split_kept(rotated)
    grad_zero = product_left(zero_part, zero_grad)
    grad_one = jnp.stack(
        [
            product_left(plus_one, plus_one_grad) + product_left(minus_one, minus_one_grad),
            product_left(plus_one, minus_one_grad) - product_left(minus_one, plus_one_grad),
        ]
    )
    grad_two = jnp.stack(
        [
            product_left(plus_two, plus_two_grad) + product_left(minus_two, minus_two_grad),
            product_left(plus_two, minus_two_grad) - product_left(minus_two, plus_two_grad),
        ]
    )
    grad_gate = product_left(scalar_low, gate_low)
    backward_parts = jnp.concatenate(
        [
            product_right(zero_grad, w_zero),
            product_right(plus_one_grad, w_one[0]) + product_right(minus_one_grad, w_one[1]),
            product_right(minus_one_grad, w_one[0]) - product_right(plus_one_grad, w_one[1]),
            product_right(plus_two_grad, w_two[0]) + product_right(minus_two_grad, w_two[1]),
            product_right(minus_two_grad, w_two[0]) - product_right(plus_two_grad, w_two[1]),
        ],
        axis=1,
    ).reshape(rows, -1, width)
    rotated_grad = (backward_parts * radial_rows.astype(jnp.float32)[:, None, :]).astype(
        jnp.bfloat16
    )
    source_grad = jnp.einsum(
        "kje,ekc->ejc", rotation, rotated_grad, preferred_element_type=jnp.float32
    ).astype(jnp.bfloat16)
    return (source_grad, (grad_zero, grad_one, grad_two, grad_gate))


def selector(index_row, piece):
    columns = jnp.arange(piece.shape[0], dtype=jnp.int32)
    hits = (index_row[:, None] == columns[None, :]).astype(jnp.bfloat16)
    return jnp.dot(hits, piece, preferred_element_type=jnp.float32)


def spreader(index_row, values, count_rows):
    owners = jnp.arange(count_rows, dtype=jnp.int32)
    hits = (owners[:, None] == index_row[None, :]).astype(jnp.bfloat16)
    return jnp.dot(hits, values, preferred_element_type=jnp.float32)


def per_device(
    nodes, sources, targets, edge_counts, wigner, radial, cotangent, w_zero, w_one, w_two, w_gate
):
    node_rows = nodes[0]
    source_ids = sources[0]
    target_ids = targets[0]
    live_edges = edge_counts[0, 0]
    rotation = wigner[0]
    radial_rows = radial[0]
    upstream_rows = cotangent[0]
    edge_rows = source_ids.shape[0]
    width = w_gate.shape[0]
    node_count = node_rows.shape[0]
    valid = jnp.arange(edge_rows, dtype=jnp.int32) < live_edges
    gathered = selector(source_ids, lax.all_gather(node_rows, "graph", axis=0, tiled=True))
    gathered = gathered.astype(jnp.bfloat16).reshape(edge_rows, -1, width)
    back, saved = edge_forward(gathered, rotation, radial_rows, valid, w_zero, w_one, w_two, w_gate)
    summed = lax.psum_scatter(
        spreader(
            target_ids, back.reshape(edge_rows, -1), node_count * lax.axis_size("graph")
        ).astype(jnp.bfloat16),
        "graph",
        scatter_dimension=0,
        tiled=True,
    )
    upstream = selector(target_ids, lax.all_gather(upstream_rows, "graph", axis=0, tiled=True))
    upstream = (
        (upstream * valid[:, None].astype(jnp.float32))
        .astype(jnp.bfloat16)
        .reshape(edge_rows, -1, width)
    )
    source_grad, grads = edge_backward(
        upstream, rotation, radial_rows, saved, w_zero, w_one, w_two, w_gate
    )
    grad_rows = lax.psum_scatter(
        spreader(
            source_ids, source_grad.reshape(edge_rows, -1), node_count * lax.axis_size("graph")
        ).astype(jnp.bfloat16),
        "graph",
        scatter_dimension=0,
        tiled=True,
    )
    grad_zero, grad_one, grad_two, grad_gate = lax.psum(
        (grads[0], grads[1], grads[2], grads[3]), ("dp", "graph")
    )
    return (summed[None], grad_rows[None], grad_zero, grad_one, grad_two, grad_gate)


def solution(mesh):
    in_specs = (
        P("dp", "graph", None),
        P("dp", "graph"),
        P("dp", "graph"),
        P("dp", "graph"),
        P("dp", None, None, "graph"),
        P("dp", "graph", None),
        P("dp", "graph", None),
        P(),
        P(),
        P(),
        P(),
    )
    out_specs = (P("dp", "graph", None), P("dp", "graph", None), P(), P(), P(), P())
    return jax.shard_map(
        per_device, mesh=mesh, in_specs=in_specs, out_specs=out_specs, check_vma=False
    )
```

profile of v0, /device:TPU:1, one launch (start us, length us, event | category | flops | bytes accessed | tf_op | source)
XLA Modules:
  0.0 593.8 jit_solution(413141231650881759)
XLA Ops:
  8.7 8.4 %copy.28 = bf16[29,49,512]{1,0,2:T(8,128)(2,1)} copy(bf16[29,49,512]{2,0,1:T(8,128)(2,1)} %bitcast.227) | data formatting | bytes 2910208 | tf_op jit(solution)/shard_map/squeeze | solution.py:127
  18.6 44.6 %all-gather.5.cloned.1.call-done = bf16[1,128,6272]{2,1,0:T(8,128)(2,1)} async-done(((bf16[1,16,6272]{2,1,0:T(8,128)(2,1)}), bf16[1,128,6272]{2,1,0:T(8,128)(2,1)}) %all-gather.5.cloned.1.call-update) | async-done | bytes 1605648 | tf_op jit(solution)/shard_map/all_gather | solution.py:134
  63.2 6.0 %convolution_convert_fusion = bf16[512,6272]{1,0:T(8,128)(2,1)} fusion(bf16[1,128,6272]{2,1,0:T(8,128)(2,1)} %all-gather.5.cloned.1.call-done, s32[512]{0:T(512)S(1)} %bitcast.228), kind=kOutput, calls=%fused_computation.1 | convolution fusion | flops 825360384 | bytes 8030208 | tf_op jit(solution)/shard_map/dot_general | solution.py:111
  69.2 9.3 %copy.26 = bf16[512,6272]{0,1:T(8,128)(2,1)} copy(bf16[512,6272]{1,0:T(8,128)(2,1)} %convolution_convert_fusion) | data formatting | bytes 12845056 | tf_op jit(solution)/shard_map/convert_element_type | solution.py:135
  78.5 10.8 %copy.27 = bf16[512,49,128]{2,1,0:T(8,128)(2,1)} copy(bf16[512,49,128]{0,2,1:T(8,128)(2,1)} %bitcast.189) | data formatting | bytes 12845056 | tf_op jit(solution)/shard_map/reshape | solution.py:135
  89.3 8.4 %fusion.1 = bf16[512,29,128]{2,1,0:T(8,128)(2,1)} fusion(f32[512,128]{1,0:T(8,128)S(1)} %bitcast_convert_fusion.1, bf16[512,49,128]{2,1,0:T(8,128)(2,1)} %copy.27, bf16[29,49,512]{1,0,2:T(8,128)(2,1)} %copy.28), kind=kOutput, calls=%fused_computation.14 | convolution fusion | flops 190054400 | bytes 11940864 | tf_op jit(solution)/shard_map/kje,ejc->ekc/dot_general | solution.py:32
  97.7 4.4 fusion.69
  105.3 2.3 copy.30
  109.1 2.3 copy.32
  113.5 2.4 fusion.36
  115.9 2.1 fusion.28
  119.7 2.6 convolution_dynamic-update-slice_fusion.1
  124.3 2.1 add_dynamic-update-slice_fusion.1
  130.2 8.8 %copy.34 = f32[512,3712]{0,1:T(8,128)} copy(f32[512,3712]{1,0:T(8,128)} %fusion.7) | data formatting | bytes 15204352 | tf_op jit(solution)/shard_map/concatenate | solution.py:35
  139.0 7.5 %slice.102 = f32[512,28,128]{0,2,1:T(8,128)} slice(f32[512,29,128]{0,2,1:T(8,128)} %bitcast.184), slice={[0:512], [1:29], [0:128]} | slice | bytes 14680064 | tf_op jit(solution)/shard_map/slice | solution.py:49
  147.5 8.4 %copy.57 = f32[512,28,128]{2,0,1:T(8,128)} copy(f32[512,28,128]{0,2,1:T(8,128)} %slice.102) | data formatting | bytes 14680064
  155.8 6.0 %multiply_convert_fusion = bf16[512,6272]{1,0:T(8,128)(2,1)} fusion(f32[512]{0:T(512)S(1)} %fusion.65, bf16[1,128,6272]{2,1,0:T(8,128)(2,1)} %all-gather.7.cloned.1.call-done, s32[512]{0:T(512)S(1)} %bitcast.230), kind=kOutput, calls=%fused_computation | convolution fusion | flops 828571648 | bytes 8032256 | tf_op jit(solution)/shard_map/dot_general | solution.py:111
  161.8 9.4 %copy.40 = bf16[512,6272]{0,1:T(8,128)(2,1)} copy(bf16[512,6272]{1,0:T(8,128)(2,1)} %multiply_convert_fusion) | data formatting | bytes 12845056 | tf_op jit(solution)/shard_map/convert_element_type | solution.py:148
  171.2 10.9 %copy.41 = bf16[512,49,128]{2,1,0:T(8,128)(2,1)} copy(bf16[512,49,128]{0,2,1:T(8,128)(2,1)} %bitcast.190) | data formatting | bytes 12845056 | tf_op jit(solution)/shard_map/reshape | solution.py:149
  182.1 9.7 %fusion.77 = f32[512,128,29]{1,2,0:T(8,128)} fusion(bf16[512,49,128]{2,1,0:T(8,128)(2,1)} %copy.41, bf16[29,49,512]{1,0,2:T(8,128)(2,1)} %copy.28), kind=kOutput, calls=%fused_computation.117 | convolution fusion | flops 186253312 | bytes 15479808 | tf_op jit(solution)/shard_map/kje,ejc->ekc/dot_general | solution.py:62
  191.9 10.8 %copy.61 = f32[512,128,29]{1,0,2:T(8,128)} copy(f32[512,128,29]{1,2,0:T(8,128)} %fusion.77) | data formatting | bytes 15204352 | tf_op jit(solution)/shard_map/kje,ejc->ekc/dot_general | solution.py:62
  203.1 7.0 %multiply_reduce_fusion = (f32[512,128]{1,0:T(8,128)}, bf16[512,28,128]{2,0,1:T(8,128)(2,1)S(1)}, f32[512,28,128]{2,0,1:T(8,128)S(1)}) fusion(f32[512,28,128]{2,0,1:T(8,128)} %copy.57, f32[512,29,128]{2,0,1:T(8,128)} %bitcast.187, f32[512,128]{1,0:T(8,128)S(1)} %fusion.23), kind=kLoop, calls=%fused_computation.11 | loop fusion | flops 9109504 | bytes 26214400 | tf_op jit(solution)/shard_map/reduce_sum | solution.py:66
  212.9 2.5 fusion
  216.4 9.1 %convert_bitcast_fusion.1 = bf16[512,49,128]{2,1,0:T(8,128)(2,1)} fusion(bf16[29,49,512]{1,0,2:T(8,128)(2,1)S(1)} %copy-done.1, bf16[512,29,128]{2,0,1:T(8,128)(2,1)} %fusion), kind=kOutput, calls=%fused_computation.12 | convolution fusion | flops 189464576 | bytes 11678720 | tf_op jit(solution)/shard_map/kje,ekc->ejc/dot_general | solution.py:52
  225.5 12.2 %copy.39 = bf16[512,49,128]{0,2,1:T(8,128)(2,1)} copy(bf16[512,49,128]{2,1,0:T(8,128)(2,1)} %convert_bitcast_fusion.1) | data formatting | bytes 12845056 | tf_op jit(solution)/shard_map/convert_element_type | solution.py:52
  237.7 6.3 %convolution_convert_fusion.2 = bf16[128,6272]{1,0:T(8,128)(2,1)} fusion(bf16[512,6272]{0,1:T(8,128)(2,1)} %bitcast.182, s32[512]{0:T(512)S(1)} %bitcast.231), kind=kOutput, calls=%fused_computation.3 | convolution fusion | flops 822951936 | bytes 8030208 | tf_op jit(solution)/shard_map/dot_general | solution.py:117
  245.3 2.1 pad_maximum_fusion.2
  249.3 2.6 convolution_dynamic-update-slice_fusion
  253.4 3.5 fusion.16
  256.9 2.3 copy.47
  259.2 3.5 fusion.14
  264.1 3.3 fusion.33
  267.4 2.2 copy.49
  269.5 2.3 fusion.31
  271.9 3.4 add_dynamic-update-slice_fusion
  282.0 8.8 %copy.50 = f32[512,3712]{0,1:T(8,128)} copy(f32[512,3712]{1,0:T(8,128)} %fusion.5) | data formatting | bytes 15204352 | tf_op jit(solution)/shard_map/concatenate | solution.py:89
  290.8 6.2 %multiply_convert_fusion.2 = bf16[512,29,128]{0,2,1:T(8,128)(2,1)} fusion(f32[512,29,128]{0,2,1:T(8,128)} %bitcast.186, f32[512,128]{0,1:T(8,128)S(1)} %copy-done.37), kind=kLoop, calls=%fused_computation.8 | loop fusion | flops 3801088 | bytes 11665408 | tf_op jit(solution)/shard_map/convert_element_type | solution.py:99
  297.0 8.1 %copy.52 = bf16[512,29,128]{2,1,0:T(8,128)(2,1)} copy(bf16[512,29,128]{0,2,1:T(8,128)(2,1)} %multiply_convert_fusion.2) | data formatting | bytes 7602176 | tf_op jit(solution)/shard_map/convert_element_type | solution.py:99
  305.0 10.4 %convert_bitcast_fusion = bf16[512,49,128]{2,1,0:T(8,128)(2,1)} fusion(bf16[512,29,128]{2,1,0:T(8,128)(2,1)} %copy.52, bf16[29,49,512]{1,0,2:T(8,128)(2,1)} %copy.28), kind=kOutput, calls=%fused_computation.9 | convolution fusion | flops 189464576 | bytes 11678720 | tf_op jit(solution)/shard_map/kje,ekc->ejc/dot_general | solution.py:102
  315.5 12.2 %copy.54 = bf16[512,49,128]{0,2,1:T(8,128)(2,1)} copy(bf16[512,49,128]{2,1,0:T(8,128)(2,1)} %convert_bitcast_fusion) | data formatting | bytes 12845056 | tf_op jit(solution)/shard_map/convert_element_type | solution.py:104
  327.6 6.2 %convolution_convert_fusion.1 = bf16[128,6272]{1,0:T(8,128)(2,1)} fusion(bf16[512,6272]{0,1:T(8,128)(2,1)} %bitcast.183, s32[512]{0:T(512)S(1)} %bitcast.229), kind=kOutput, calls=%fused_computation.2 | convolution fusion | flops 822951936 | bytes 8030208 | tf_op jit(solution)/shard_map/dot_general | solution.py:117
  333.9 2.1 fusion.82
  343.8 2.5 pad_maximum_fusion
  347.2 2.8 fusion.78
  350.1 53.8 %reduce-scatter.5.cloned.1.call-done = bf16[16,6272]{1,0:T(8,128)(2,1)} async-done(((bf16[128,6272]{1,0:T(8,128)(2,1)}), bf16[16,6272]{1,0:T(8,128)(2,1)}) %reduce-scatter.5.cloned.1.call-update) | async-done | bytes 200720 | tf_op jit(solution)/shard_map/reduce_scatter | solution.py:154
  403.9 173.3 %all-reduce.3.cloned.1.call-done = (f32[896,896]{1,0:T(8,128)}, f32[2,768,768]{2,1,0:T(8,128)}, f32[2,640,640]{2,1,0:T(8,128)}, f32[128,128]{1,0:T(8,128)}) async-done(((f32[896,896]{1,0:T(8,128)}, f32[2,768,768]{2,1,0:T(8,128)}, f32[2,640,640]{2,1,0:T(8,128)}, f32[128,128]{1,0:T(8,128)}), (f32[896,896]{1,0:T(8,128)}, f32[2,768,768]{2,1,0:T(8,128)}, f32[2,640,640]{2,1,0:T(8,128)}, ...) | async-done | bytes 11272208 | tf_op jit(solution)/shard_map/psum | solution.py:162
  577.2 3.9 copy.75
  581.1 2.4 copy.76
  (139 shorter events, 46.5 us)
Async XLA Ops:
  7.2 112.5 %copy-start = (bf16[896,896]{1,0:T(8,128)(2,1)S(1)}, bf16[896,896]{1,0:T(8,128)(2,1)}, u32[]{:S(2)}) copy-start(bf16[896,896]{1,0:T(8,128)(2,1)} %param.18) | copy-start | bytes 4816900
  7.2 9.9 %copy-start.39 = (bf16[1,512,128]{2,1,0:T(8,128)(2,1)S(1)}, bf16[1,512,128]{2,1,0:T(8,128)(2,1)}, u32[]{:S(2)}) copy-start(bf16[1,512,128]{2,1,0:T(8,128)(2,1)} %param.16) | copy-start | bytes 393220
  7.2 56.0 %all-gather.5.cloned.1.call-start = ((), (), s32[]{:S(2)}) async-start(), calls=%async_computation.4 | async-start | bytes 1806336 | tf_op jit(solution)/shard_map/all_gather | solution.py:134
  7.9 147.9 %all-gather.7.cloned.1.call-start = ((), (), s32[]{:S(2)}) async-start(), calls=%async_computation.5 | async-start | bytes 1806336 | tf_op jit(solution)/shard_map/all_gather | solution.py:145
  8.7 341.4 %reduce-scatter.3.cloned.1.call-start = ((), (), s32[]{:S(2)}) async-start(), calls=%async_computation.2 | async-start | bytes 1806336 | tf_op jit(solution)/shard_map/reduce_scatter | solution.py:137
  8.7 54.5 %copy-start.38 = (s32[1,512]{1,0:T(1,128)S(1)}, s32[1,512]{1,0:T(1,128)}, u32[]{:S(2)}) copy-start(s32[1,512]{1,0:T(1,128)} %param.12) | copy-start | bytes 6148
  97.7 4.4 copy-start.3
  97.7 6.1 %slice-start = ((bf16[512,29,128]{2,1,0:T(8,128)(2,1)}), bf16[512,7,128]{2,1,0:T(8,128)(2,1)S(1)}, s32[]{:S(2)}) async-start(bf16[512,29,128]{2,1,0:T(8,128)(2,1)} %fusion.1), calls=%async_computation.7 | async-start | bytes 2097152 | tf_op jit(solution)/shard_map/slice | solution.py:26
  113.5 14.9 %copy-start.4 = (bf16[512,5,128]{0,2,1:T(8,128)(2,1)}, bf16[512,5,128]{0,2,1:T(8,128)(2,1)S(1)}, u32[]{:S(2)}) copy-start(bf16[512,5,128]{0,2,1:T(8,128)(2,1)S(1)} %copy.33) | copy-start | bytes 1966084
  113.5 4.6 copy-start.17
  113.5 4.6 copy-start.19
  118.1 1.7 copy-start.26
  124.3 2.1 copy-start.10
  147.4 8.4 %copy-start.40 = (s32[1,512]{1,0:T(1,128)S(1)}, s32[1,512]{1,0:T(1,128)}, u32[]{:S(2)}) copy-start(s32[1,512]{1,0:T(1,128)} %param.13) | copy-start | bytes 6148
  191.9 11.0 %copy-start.42 = (bf16[128,128]{1,0:T(8,128)(2,1)S(1)}, bf16[128,128]{1,0:T(8,128)(2,1)}, u32[]{:S(2)}) copy-start(bf16[128,128]{1,0:T(8,128)(2,1)} %param.21) | copy-start | bytes 98308
  202.8 7.3 %copy-start.29 = (f32[512,1,128]{2,0,1:T(8,128)}, f32[512,1,128]{2,0,1:T(8,128)S(1)}, u32[]{:S(2)}) copy-start(f32[512,1,128]{2,0,1:T(8,128)S(1)} %copy.56) | copy-start | bytes 786436
  203.1 7.0 %copy-start.34 = (f32[512,128]{1,0:T(8,128)}, f32[512,128]{1,0:T(8,128)S(1)}, u32[]{:S(2)}) copy-start(f32[512,128]{1,0:T(8,128)S(1)} %fusion.23) | copy-start | bytes 786436
  210.1 2.8 copy-start.2
  212.8 3.6 copy-start.1
  237.7 6.4 %copy-start.35 = (f32[512,128]{1,0:T(8,128)S(1)}, f32[512,128]{1,0:T(8,128)}, u32[]{:S(2)}) copy-start(f32[512,128]{1,0:T(8,128)} %copy-done.34) | copy-start | bytes 786436
  237.7 6.4 %copy-start.36 = (f32[512,128]{1,0:T(8,128)S(1)}, f32[512,128]{1,0:T(8,128)}, u32[]{:S(2)}) copy-start(f32[512,128]{1,0:T(8,128)} %get-tuple-element.10) | copy-start | bytes 786436
  237.7 6.4 %copy-start.30 = (f32[512,1,128]{2,0,1:T(8,128)S(1)}, f32[512,1,128]{2,0,1:T(8,128)}, u32[]{:S(2)}) copy-start(f32[512,1,128]{2,0,1:T(8,128)} %copy-done.29) | copy-start | bytes 786436
  237.7 6.4 %copy-start.43 = (bf16[128,128]{1,0:T(8,128)(2,1)S(1)}, bf16[128,128]{1,0:T(8,128)(2,1)}, u32[]{:S(2)}) copy-start(bf16[128,128]{1,0:T(8,128)(2,1)} %param.21) | copy-start | bytes 98308
  244.0 159.8 %reduce-scatter.5.cloned.1.call-start = ((), (), s32[]{:S(2)}) async-start(), calls=%async_computation.3 | async-start | bytes 1806336 | tf_op jit(solution)/shard_map/reduce_scatter | solution.py:154
  249.3 2.6 copy-start.24
  253.3 9.3 %copy-start.12 = (bf16[512,6,128]{0,2,1:T(8,128)(2,1)}, bf16[512,6,128]{0,2,1:T(8,128)(2,1)S(1)}, u32[]{:S(2)}) copy-start(bf16[512,6,128]{0,2,1:T(8,128)(2,1)S(1)} %copy.46) | copy-start | bytes 2359300
  264.0 15.9 %copy-start.6 = (bf16[512,5,128]{0,2,1:T(8,128)(2,1)}, bf16[512,5,128]{0,2,1:T(8,128)(2,1)S(1)}, u32[]{:S(2)}) copy-start(bf16[512,5,128]{0,2,1:T(8,128)(2,1)S(1)} %copy.48) | copy-start | bytes 1966084
  269.5 2.3 copy-start.15
  269.5 2.3 copy-start.32
  271.9 3.5 copy-start.13
  271.9 3.5 copy-start.18
  271.9 3.5 copy-start.33
  275.3 2.1 copy-start.8
  275.3 2.0 copy-start.11
  275.4 2.6 copy-start.22
  282.0 8.8 %copy-start.37 = (f32[512,128]{0,1:T(8,128)S(1)}, f32[512,128]{0,1:T(8,128)}, u32[]{:S(2)}) copy-start(f32[512,128]{0,1:T(8,128)} %copy.51) | copy-start | bytes 786436
  333.8 2.2 copy-start.5
  333.9 243.3 %all-reduce.3.cloned.1.call-start = ((), (), s32[]{:S(2)}) async-start(), calls=%async_computation.6 | async-start | bytes 22544384 | tf_op jit(solution)/shard_map/psum | solution.py:162
  333.9 2.2 copy-start.7
  333.9 2.9 copy-start.21
  338.2 1.9 copy-start.16
  338.3 1.9 copy-start.20
  343.8 2.5 copy-start.31
  343.8 3.4 copy-start.25
  343.8 3.4 copy-start.27
  577.2 4.0 copy-start.23
  581.1 3.6 copy-start.28
  584.7 1.7 copy-start.41
  (2 other events, 2.6 us)
Sparse Core Ops, SparseCore 0:
  10.3 52.8 all-gather.4
  65.5 49.8 all-gather.6
  244.2 69.9 reduce-scatter.2
  334.0 69.8 reduce-scatter.4
  409.9 167.1 all-reduce.2
where the time goes:
time: 603 us; the launch traced here: 594 us
  waiting for transfers between devices  273 us (45%)
  local copies, waits for them, and re-layouts  167 us (28%)
  matrix products  116 us (19%)
  other arithmetic  22.4 us (4%)
  between operations  15.2 us (3%)
    psum x1, waiting for transfers between devices, per_device(): lax.psum((grads[0], grads[1], grads[2], grads[3]), ('dp', 'graph'))  173 us
    reduce_scatter x1, waiting for transfers between devices, per_device(): lax.psum_scatter(spreader(source_ids, source_grad.reshape(edge_rows, -1),...  53.8 us
    all_gather x1, waiting for transfers between devices, per_device(): lax.all_gather(node_rows, 'graph', axis=0, tiled=True)  44.6 us
    slice x16, local copies, waits for them, and re-layouts, split_kept(): values[:, lower:upper, :].reshape(rows, -1)  27.5 us
    dot_general x10, matrix products, product_right(): lax.dot_general(left, right, (((1,), (1,)), ((), ())), preferred_element_...  25.8 us
    unnamed x94, local copies, waits for them, and re-layouts  20.5 us
    dot_general x10, matrix products, product(): return jnp.dot(left, right, preferred_element_type=jnp.float32)  16.9 us
    dot_general x2, matrix products, spreader(): return jnp.dot(hits, values, preferred_element_type=jnp.float32)  12.5 us
  transfers between devices with their start and end apart: 5, of which 3 were waited for; matrix products, arithmetic and copies ran while one was open for 35% of the time, Pallas kernels for 0%

commit v1 on v0

v1 whole, which is shorter than its diff:
```python
import jax
import jax.numpy as jnp
from jax import lax
from jax.experimental import pallas as pl
from jax.experimental.pallas import tpu as pltpu
from jax.sharding import PartitionSpec as P

BF = jnp.bfloat16
F32 = jnp.float32
C = 128
CH = 32
ONE_AT, TWO_AT, GATE_AT, USED, TOTAL = 6272, 15488, 21888, 22016, 22528


def kept(l):
    ks = [l]
    if l >= 1:
        ks += [7 + l - 1, 13 + l - 1]
    if l >= 2:
        ks += [19 + l - 2, 24 + l - 2]
    return ks


def nn(a, b):
    return jnp.dot(a, b, preferred_element_type=F32)


def nt(a, b):
    return lax.dot_general(a, b, (((1,), (1,)), ((), ())), preferred_element_type=F32)


def tn(a, b):
    return lax.dot_general(a, b, (((0,), (0,)), ((), ())), preferred_element_type=F32)


def weighted(terms):
    total = None
    for w, v in terms:
        part = v.reshape(CH // 8, 8, 128) * w[None]
        total = part if total is None else total + part
    return total.reshape(CH, 128)


def prepare(src, tgt, cnt, wig, rad, w0, w1, w2, wg, w0t, w1t, w2t, wgt, wf, radt, ohs, oht):
    edges = src.shape[1]

    def spread_row(k, _):
        for q in range(4):
            wf[q, k, 0:49, :] = wig[k, :, q * 128 : (q + 1) * 128].astype(F32)
        return 0

    lax.fori_loop(0, 29, spread_row, 0)
    node = lax.broadcasted_iota(jnp.int32, (128, edges), 0)
    slot = lax.broadcasted_iota(jnp.int32, (128, edges), 1)
    ohs[...] = jnp.where(node == src[...], 1.0, 0.0).astype(BF)
    live = slot < cnt[...]
    oht[...] = jnp.where((node == tgt[...]) & live, 1.0, 0.0).astype(BF)
    radt[...] = rad[...].astype(F32).T

    def turn(block, out, size):
        def step(i, _):
            at = pl.multiple_of(i * 128, 128)
            out[:, pl.ds(at, 128)] = block[pl.ds(at, 128), :].T
            return 0

        lax.fori_loop(0, size // 128, step, 0)

    turn(w0, w0t, 896)
    for i in range(2):
        turn(w1.at[i], w1t.at[i], 768)
        turn(w2.at[i], w2t.at[i], 640)
    wgt[...] = wg[...].T


INTERPRET = False


def row(wf, q, k, j):
    if INTERPRET:
        return jnp.broadcast_to(wf[q, k, pl.ds(j, 1), :], (8, 128))
    return wf[q, k, pl.ds(j, 8, stride=0), :]


def tiles(body):
    def step(t, _):
        body(pl.multiple_of((t // 4) * CH, CH), t % 4)
        return 0

    lax.fori_loop(0, 4 * (128 // CH), step, 0)


def turn_in(l, wf, gbuf, emit):
    count = 2 * l + 1

    def body(c0, q):
        e0 = pl.multiple_of(q * 128, 128)
        vals = [gbuf[pl.ds(j * 128 + c0, CH), pl.ds(e0, 128)].astype(F32) for j in range(count)]
        for k in kept(l):
            emit(k, weighted([(row(wf, q, k, l * l + j), vals[j]) for j in range(count)]), c0, e0)

    tiles(body)


def turn_out(l, wf, load, bk):
    count = 2 * l + 1

    def body(c0, q):
        e0 = pl.multiple_of(q * 128, 128)
        vals = [load(k, c0, e0) for k in kept(l)]
        for j in range(count):
            out = weighted([(row(wf, q, k, l * l + j), v) for k, v in zip(kept(l), vals)])
            bk[pl.ds(j * 128 + c0, CH), pl.ds(e0, 128)] = out.astype(BF)

    tiles(body)


def halves(body):
    def step(h, _):
        body(pl.ds(pl.multiple_of(h * 256, 256), 256))
        return 0

    lax.fori_loop(0, 2, step, 0)


def sigmoid(v):
    return 1.0 / (1.0 + jnp.exp(-v))


def cols(l):
    return slice(l * l * 128, (l + 1) * (l + 1) * 128)


def forward(nodes, wf, radt, ohs, w0t, w1t, w2t, wgt, gbuf, R, mix, gate):
    for l in range(7):
        gbuf[0 : (2 * l + 1) * 128, :] = tn(nodes[:, cols(l)], ohs[...]).astype(BF)

        def emit(k, v, c0, e0):
            R[pl.ds(k * 128 + c0, CH), pl.ds(e0, 128)] = (v * radt[pl.ds(c0, CH), pl.ds(e0, 128)]).astype(BF)

        turn_in(l, wf, gbuf, emit)

    def zero(e):
        mix[0:896, e] = nn(w0t[...], R[0:896, e])
        scalar = mix[0:128, e].astype(BF)
        gate[:, e] = sigmoid(nn(wgt[...], scalar))

    halves(zero)
    for wt, at, n in ((w1t, 896, 768), (w2t, 2432, 640)):
        def pair(e):
            p, m = R[at : at + n, e], R[at + n : at + 2 * n, e]
            mix[at : at + n, e] = nn(wt[0], p) - nn(wt[1], m)
            mix[at + n : at + 2 * n, e] = nn(wt[1], p) + nn(wt[0], m)

        halves(pair)


def send_messages(wf, mix, gate, oht, bk, agg):
    for l in range(7):
        def load(k, c0, e0):
            v = mix[pl.ds(k * 128 + c0, CH), pl.ds(e0, 128)]
            m = v * sigmoid(v) if k == 0 else v * gate[pl.ds(c0, CH), pl.ds(e0, 128)]
            return m.astype(BF).astype(F32)

        turn_out(l, wf, load, bk)
        agg[:, cols(l)] = nt(oht[...], bk[0 : (2 * l + 1) * 128, :]).astype(BF)


def backward(cot, wf, oht, wg, gbuf, mix, gate, G, gl, direct):
    gl[...] = jnp.zeros_like(gl)
    for l in range(7):
        gbuf[0 : (2 * l + 1) * 128, :] = tn(cot[:, cols(l)], oht[...]).astype(BF)

        def emit(k, v, c0, e0):
            at = (pl.ds(c0, CH), pl.ds(e0, 128))
            x = mix[pl.ds(k * 128 + c0, CH), pl.ds(e0, 128)]
            if k == 0:
                s = sigmoid(x)
                direct[at] = v * s * (1.0 + x * (1.0 - s))
            else:
                G[pl.ds(k * 128 + c0, CH), pl.ds(e0, 128)] = (v * gate[at]).astype(BF)
                gl[at] += v * x

        turn_in(l, wf, gbuf, emit)
    low = (gl[...] * gate[...] * (1.0 - gate[...])).astype(BF)
    G[0:128, :] = (direct[...] + nn(wg[...], low)).astype(BF)
    return low


def weight_grads(R, G, mix, low, g):
    for at in (0, 256, 512, 768):
        wide = min(256, 896 - at)
        out = nt(R[0:896, :], G[at : at + wide, :]).astype(BF)
        for q in range(wide // 128):
            p = at // 128 + q
            g[p * 896 : (p + 1) * 896, :] = out[:, q * 128 : (q + 1) * 128]
    for base, at, n in ((ONE_AT, 896, 768), (TWO_AT, 2432, 640)):
        for lo in range(0, n, 256):
            wide = min(256, n - lo)
            plus, minus = G[at + lo : at + lo + wide, :], G[at + n + lo : at + n + lo + wide, :]
            rp, rm = R[at : at + n, :], R[at + n : at + 2 * n, :]
            for i, out in enumerate((nt(rp, plus) + nt(rm, minus), nt(rp, minus) - nt(rm, plus))):
                out = out.astype(BF)
                for q in range(wide // 128):
                    r = base + (i * (n // 128) + lo // 128 + q) * n
                    g[r : r + n, :] = out[:, q * 128 : (q + 1) * 128]
    g[GATE_AT:USED, :] = nt(mix[0:128, :].astype(BF), low).astype(BF)
    g[USED:TOTAL, :] = jnp.zeros((TOTAL - USED, 128), BF)


def rotated_grads(radt, w0, w1, w2, G, R):
    def scale(v, e):
        n = v.shape[0]
        return (v.reshape(n // 128, 128, v.shape[1]) * radt[:, e][None]).reshape(v.shape).astype(BF)

    def zero(e):
        R[0:896, e] = scale(nn(w0[...], G[0:896, e]), e)

    halves(zero)
    for w, at, n in ((w1, 896, 768), (w2, 2432, 640)):
        def pair(e):
            p, m = G[at : at + n, e], G[at + n : at + 2 * n, e]
            R[at : at + n, e] = scale(nn(w[0], p) + nn(w[1], m), e)
            R[at + n : at + 2 * n, e] = scale(nn(w[0], m) - nn(w[1], p), e)

        halves(pair)


def source_grads(wf, ohs, R, bk, gn):
    for l in range(7):
        def load(k, c0, e0):
            return R[pl.ds(k * 128 + c0, CH), pl.ds(e0, 128)].astype(F32)

        turn_out(l, wf, load, bk)
        gn[:, cols(l)] = nt(ohs[...], bk[0 : (2 * l + 1) * 128, :]).astype(BF)


HALF = TOTAL // 2
MESH = pl.DeviceIdType.MESH
PEERS = [(dz, dy) for dz in range(2) for dy in range(4) if (dz, dy) != (0, 0)]
COLORS = ((0, 4096, (0, 1, 2)), (4096, 4096, (1, 2, 0)), (8192, 3072, (2, 0, 1)))
SLOT_ROWS = sum(3 * (size // 4 + size // 16 + size // 64) for _, size, _ in COLORS)
N_SEMS = 4 * 7 + 2 + 2 * 27


class Links:
    def __init__(self, send, recv):
        dp, self.g = lax.axis_index("dp"), lax.axis_index("graph")
        self.dp = dp
        self.pos = (dp // 4, self.g % 4, (self.g // 4) * 2 + (dp // 2) % 2)
        self.core = dp % 2
        self.send, self.recv, self.used = send, recv, 0

    def at(self, x, y, z, core):
        return ((x * 2 + z % 2) * 2 + core, (z // 2) * 4 + y)

    def along(self, axis, step):
        pos = list(self.pos)
        pos[axis] = (pos[axis] + step) % 4
        return self.at(*pos, self.core)

    def graph_peer(self, dz, dy):
        return (self.dp, ((self.g // 4 + dz) % 2) * 4 + (self.g % 4 + dy) % 4)

    def other_core(self):
        return self.at(*self.pos, 1 - self.core)

    def greet(self):
        peers = [self.graph_peer(*p) for p in PEERS]
        peers += [self.along(0, 1), self.along(0, 2), self.along(0, 3), self.along(2, 1), self.along(2, 3)]
        peers.append(self.other_core())
        barrier = pltpu.get_barrier_semaphore()
        for peer in peers:
            pl.semaphore_signal(barrier, inc=1, device_id=peer, device_id_type=MESH)
        pl.semaphore_wait(barrier, len(peers))

    def copy(self, src, dst, peer):
        out = pltpu.make_async_remote_copy(
            src_ref=src, dst_ref=dst, send_sem=self.send.at[self.used], recv_sem=self.recv.at[self.used],
            device_id=peer, device_id_type=MESH,
        )
        self.used += 1
        out.start()
        return out


def done(copies):
    for c in copies:
        c.wait()


def rows16(i, n=16):
    return pl.ds(pl.multiple_of(i * 16, 16), n)


def gather_start(links, x, full):
    mine = rows16(links.g)
    out = [links.copy(x, full.at[mine], links.graph_peer(*p)) for p in PEERS]
    full[mine, :] = x[...]
    return out


def scatter_start(links, part, slots):
    out = []
    for i, p in enumerate(PEERS):
        peer = links.graph_peer(*p)
        out.append(links.copy(part.at[rows16(peer[1])], slots.at[i], peer))
    return out


def scatter_finish(links, copies, part, slots, out):
    done(copies)
    total = part[rows16(links.g), :].astype(F32)
    for i in range(len(PEERS)):
        total += slots[i].astype(F32)
    out[...] = total.astype(BF)


def add_rows(dst, d0, srcs, n):
    step = 256 if n % 256 == 0 else n

    def body(t, _):
        total = None
        for ref, r in srcs:
            v = ref[pl.ds(pl.multiple_of(r + t * step, 16), step), :].astype(F32)
            total = v if total is None else total + v
        dst[pl.ds(pl.multiple_of(d0 + t * step, 16), step), :] = total.astype(BF)
        return 0

    if n == step:
        body(0, 0)
    else:
        lax.fori_loop(0, n // step, body, 0)


def swap_start(links, g, inbox):
    away = pl.multiple_of((1 - links.core) * HALF, 16)
    return [links.copy(g.at[pl.ds(away, HALF)], inbox, links.other_core())]


def reduce_all(links, swap, g, inbox, slots, mid, small, full):
    home = links.core * HALF
    done(swap)
    add_rows(g, home, [(g, home), (inbox, 0)], HALF)
    waiting, src, at = {}, {}, 0
    for c, (base, size, axes) in enumerate(COLORS):
        src[c] = (g, home + base)
    slot_at, place = {}, {}
    for c, (base, size, axes) in enumerate(COLORS):
        for s in range(3):
            slot_at[c, s] = at
            at += 3 * (size // 4 ** (s + 1))

    def start(c, s):
        base, size, axes = COLORS[c]
        n, (ref, row), axis = size // 4 ** (s + 1), src[c], axes[s]
        out = []
        for d in (1, 3, 2):
            j = (links.pos[axis] + d) % 4
            out.append(links.copy(
                ref.at[pl.ds(pl.multiple_of(row + j * n, 16), n)],
                slots.at[pl.ds(slot_at[c, s] + (d - 1) * n, n)],
                links.along(axis, d)))
        waiting[c] = out

    def reduce(c, s):
        base, size, axes = COLORS[c]
        n, (ref, row), axis = size // 4 ** (s + 1), src[c], axes[s]
        own = row + links.pos[axis] * n
        place[c] = place.get(c, home + base) + links.pos[axis] * n
        done(waiting[c])
        srcs = [(ref, own)] + [(slots, slot_at[c, s] + d * n) for d in range(3)]
        if s == 0:
            dst, d0 = mid, base // 4
        elif s == 1:
            dst, d0 = small, base // 16
        else:
            dst, d0 = full, place[c]
        add_rows(dst, d0, srcs, n)
        src[c] = (dst, d0)

    def share(c, s):
        base, size, axes = COLORS[c]
        n, axis = size // 4 ** (s + 1), axes[s]
        rows = pl.ds(pl.multiple_of(place[c], 16), n)
        waiting[c] = [links.copy(full.at[rows], full.at[rows], links.along(axis, d)) for d in (1, 3, 2)]
        place[c] = place[c] - links.pos[axis] * n

    for c in range(3):
        start(c, 0)
    for s in range(3):
        for c in range(3):
            reduce(c, s)
            if s < 2:
                start(c, s + 1)
            else:
                share(c, 2)
    for s in (1, 0):
        for c in range(3):
            done(waiting[c])
            share(c, s)
    for c in range(3):
        done(waiting[c])
    mine = pl.ds(pl.multiple_of(home, 16), HALF)
    done([links.copy(full.at[mine], full.at[mine], links.other_core())])


def layer_kernel(x, cx, src, tgt, cnt, wig, rad, w0, w1, w2, wg, agg, gn, full,
                 nodes, cot, w0t, w1t, w2t, wgt, wf, radt, ohs, oht, gbuf, R, mix, G, gate, gl, direct, bk,
                 pagg, slots1, slots2, g, inbox, slots, mid, small, send, recv):
    links = Links(send, recv)
    links.greet()
    arriving = gather_start(links, x, nodes)
    prepare(src, tgt, cnt, wig, rad, w0, w1, w2, wg, w0t, w1t, w2t, wgt, wf, radt, ohs, oht)
    done(arriving)
    arriving = gather_start(links, cx, cot)
    forward(nodes, wf, radt, ohs, w0t, w1t, w2t, wgt, gbuf, R, mix, gate)
    send_messages(wf, mix, gate, oht, bk, pagg)
    done(arriving)
    leaving = scatter_start(links, pagg, slots1)
    low = backward(cot, wf, oht, wg, gbuf, mix, gate, G, gl, direct)
    weight_grads(R, G, mix, low, g)
    swap = swap_start(links, g, inbox)
    scatter_finish(links, leaving, pagg, slots1, agg)
    rotated_grads(radt, w0, w1, w2, G, R)
    source_grads(wf, ohs, R, bk, nodes)
    leaving = scatter_start(links, nodes, slots2)
    reduce_all(links, swap, g, inbox, slots, mid, small, full)
    scatter_finish(links, leaving, nodes, slots2, gn)


def unpack_kernel(full, zero, one, two, last, b0, b1, b2, b3, sems):
    for p in range(7):
        b0[:, p * 128 : (p + 1) * 128] = full[p * 896 : (p + 1) * 896, :].astype(F32)
    copies = [pltpu.make_async_copy(b0, zero, sems.at[0])]
    copies[0].start()
    for buf, out, base, n, s in ((b1, one, ONE_AT, 768, 1), (b2, two, TWO_AT, 640, 3)):
        for i in range(2):
            for p in range(n // 128):
                at = base + (i * (n // 128) + p) * n
                buf[i, :, p * 128 : (p + 1) * 128] = full[at : at + n, :].astype(F32)
            copies.append(pltpu.make_async_copy(buf.at[i], out.at[i], sems.at[s + i]))
            copies[-1].start()
    b3[...] = full[GATE_AT:USED, :].astype(F32)
    copies.append(pltpu.make_async_copy(b3, last, sems.at[5]))
    copies[-1].start()
    for c in copies:
        c.wait()


def per_device(nodes, sources, targets, counts, wigner, radial, cotangent, w0, w1, w2, wg):
    vm = pl.BlockSpec(memory_space=pltpu.VMEM)
    hbm = pl.BlockSpec(memory_space=pl.ANY)
    dma = pltpu.SemaphoreType.DMA
    agg, gn, full = pl.pallas_call(
        layer_kernel,
        out_shape=(
            jax.ShapeDtypeStruct((16, 6272), BF),
            jax.ShapeDtypeStruct((16, 6272), BF),
            jax.ShapeDtypeStruct((TOTAL, 128), BF),
        ),
        in_specs=[vm] * 11,
        out_specs=(vm, vm, vm),
        scratch_shapes=[
            pltpu.VMEM((128, 6272), BF),
            pltpu.VMEM((128, 6272), BF),
            pltpu.VMEM((896, 896), BF),
            pltpu.VMEM((2, 768, 768), BF),
            pltpu.VMEM((2, 640, 640), BF),
            pltpu.VMEM((128, 128), BF),
            pltpu.VMEM((4, 29, 56, 128), F32),
            pltpu.VMEM((128, 512), F32),
            pltpu.VMEM((128, 512), BF),
            pltpu.VMEM((128, 512), BF),
            pltpu.VMEM((13 * 128, 512), BF),
            pltpu.VMEM((3712, 512), BF),
            pltpu.VMEM((3712, 512), F32),
            pltpu.VMEM((3712, 512), BF),
            pltpu.VMEM((128, 512), F32),
            pltpu.VMEM((128, 512), F32),
            pltpu.VMEM((128, 512), F32),
            pltpu.VMEM((13 * 128, 512), BF),
            pltpu.VMEM((128, 6272), BF),
            pltpu.VMEM((7, 16, 6272), BF),
            pltpu.VMEM((7, 16, 6272), BF),
            pltpu.VMEM((TOTAL, 128), BF),
            pltpu.VMEM((HALF, 128), BF),
            pltpu.VMEM((SLOT_ROWS, 128), BF),
            pltpu.VMEM((HALF // 4, 128), BF),
            pltpu.VMEM((HALF // 16, 128), BF),
            dma((N_SEMS,)),
            dma((N_SEMS,)),
        ],
        compiler_params=pltpu.CompilerParams(
            vmem_limit_bytes=67043328, collective_id=0, has_side_effects=True
        ),
        name="edge_layer",
    )(nodes[0], cotangent[0], sources, targets, counts, wigner[0], radial[0], w0, w1, w2, wg)
    zero, one, two, last = pl.pallas_call(
        unpack_kernel,
        out_shape=(
            jax.ShapeDtypeStruct((896, 896), F32),
            jax.ShapeDtypeStruct((2, 768, 768), F32),
            jax.ShapeDtypeStruct((2, 640, 640), F32),
            jax.ShapeDtypeStruct((128, 128), F32),
        ),
        in_specs=[vm],
        out_specs=(hbm,) * 4,
        scratch_shapes=[
            pltpu.VMEM((896, 896), F32),
            pltpu.VMEM((2, 768, 768), F32),
            pltpu.VMEM((2, 640, 640), F32),
            pltpu.VMEM((128, 128), F32),
            dma((6,)),
        ],
        compiler_params=pltpu.CompilerParams(vmem_limit_bytes=40 << 20),
        name="unpack",
    )(full)
    return agg[None], gn[None], zero, one, two, last


def solution(mesh):
    in_specs = (
        P("dp", "graph", None),
        P("dp", "graph"),
        P("dp", "graph"),
        P("dp", "graph"),
        P("dp", None, None, "graph"),
        P("dp", "graph", None),
        P("dp", "graph", None),
        P(),
        P(),
        P(),
        P(),
    )
    out_specs = (P("dp", "graph", None), P("dp", "graph", None), P(), P(), P(), P())
    return jax.shard_map(
        per_device, mesh=mesh, in_specs=in_specs, out_specs=out_specs, check_vma=False
    )
```

time: 603 us -> 186 us (0.31); the launches traced: 594 us -> 186 us
  waiting for transfers between devices: 273 us -> 0 us
  Pallas kernels: 0 us -> 177 us
  local copies, waits for them, and re-layouts: 167 us -> 7.42 us
  matrix products: 116 us -> 0 us
  other arithmetic: 22.4 us -> 0 us
  between operations: 15.2 us -> 1.31 us
    pallas_call x0 -> x2, Pallas kernels: none -> 177 us  [the longest x1 172 us: per_device(): pl.pallas_call(layer_kernel, out_shape=(jax.ShapeDtypeStruct((16, 6272),...]
    psum x1 -> x0, waiting for transfers between devices: 173 us -> none  [per_device(): lax.psum((grads[0], grads[1], grads[2], grads[3]), ('dp', 'graph'))]
    dot_general x38 -> x0, matrix products: 116 us -> none  [the longest x10 25.8 us: product_right(): lax.dot_general(left, right, (((1,), (1,)), ((), ())), preferred_element_...]
    reduce_scatter x2 -> x0, waiting for transfers between devices: 53.8 us -> none  [the longest x1 53.8 us: per_device(): lax.psum_scatter(spreader(source_ids, source_grad.reshape(edge_rows, -1),...]
    convert_element_type x6 -> x0, local copies, waits for them, and re-layouts: 52 us -> none  [the longest x1 12.2 us: edge_forward(): jnp.einsum('kje,ekc->ejc', rotation, message, preferred_element_type=jnp....]
    all_gather x2 -> x0, waiting for transfers between devices: 44.6 us -> none  [the longest x1 44.6 us: per_device(): lax.all_gather(node_rows, 'graph', axis=0, tiled=True)]
    slice x18 -> x0, local copies, waits for them, and re-layouts: 35.9 us -> none  [the longest x16 27.5 us: split_kept(): values[:, lower:upper, :].reshape(rows, -1)]
    reshape x2 -> x0, local copies, waits for them, and re-layouts: 21.7 us -> none  [the longest x1 10.9 us: per_device(): upstream = (upstream * valid[:, None].astype(jnp.float32)).astype(jnp.bfl...]
  transfers between devices with their start and end apart: 5 -> 0, of which waited for: 3 -> 0; matrix products, arithmetic and copies ran while one was open for 35% -> 0% of each run, Pallas kernels for 0% -> 0%
where the time goes in v1:
time: 186 us
  Pallas kernels  177 us (95%)
  local copies, waits for them, and re-layouts  7.42 us (4%)
    pallas_call x1, Pallas kernels, per_device(): pl.pallas_call(layer_kernel, out_shape=(jax.ShapeDtypeStruct((16, 6272),...  172 us
    unnamed x9, local copies, waits for them, and re-layouts  7.42 us
    pallas_call x1, Pallas kernels, per_device(): pl.pallas_call(unpack_kernel, out_shape=(jax.ShapeDtypeStruct((896, 896),...  4.46 us

profile of v1, /device:TPU:1, one launch (start us, length us, event | category | flops | bytes accessed | tf_op | source)
XLA Modules:
  0.0 185.6 jit_solution(17459956061682895806)
XLA Ops:
  1.3 3.4 %copy.19 = bf16[1,29,49,512]{3,2,1,0:T(8,128)(2,1)} copy(bf16[1,29,49,512]{3,1,2,0:T(8,128)(2,1)} %param.15) | data formatting | bytes 2910208 | tf_op args[4]
  4.7 172.4 %edge_layer.1 = (bf16[16,6272]{1,0:T(8,128)(2,1)}, bf16[16,6272]{1,0:T(8,128)(2,1)}, bf16[22528,128]{1,0:T(8,128)(2,1)}) custom-call(bf16[16,6272]{1,0:T(8,128)(2,1)} %bitcast.9, bf16[16,6272]{1,0:T(8,128)(2,1)} %bitcast.10, s32[1,512]{1,0:T(1,128)} %src.1, s32[1,512]{1,0:T(1,128)} %tgt.1, s32[1,1]{1,0:T(1,128)S(6)} %copy.22.cnt, ...), custom_call_target="tpu_custom_call" | custom-call | tf_op jit(solution)/shard_map/edge_layer/pallas_call | solution.py:454
  177.1 0.0 copy-start
  177.2 2.6 %copy-done = bf16[22528,128]{1,0:T(8,128)(2,1)S(1)} copy-done((bf16[22528,128]{1,0:T(8,128)(2,1)S(1)}, bf16[22528,128]{1,0:T(8,128)(2,1)}, u32[]{:S(2)}) %copy-start) | copy-done | bytes 5767192
  179.8 0.0 copy-start.2
  179.8 0.0 copy-start.1
  179.8 4.5 %unpack.1 = (f32[896,896]{1,0:T(8,128)}, f32[2,768,768]{2,1,0:T(8,128)}, f32[2,640,640]{2,1,0:T(8,128)}, f32[128,128]{1,0:T(8,128)}) custom-call(bf16[22528,128]{1,0:T(8,128)(2,1)S(1)} %copy-done), custom_call_target="tpu_custom_call" | custom-call | tf_op jit(solution)/shard_map/unpack/pallas_call | solution.py:498
  184.3 0.0 copy-done.2
  184.3 0.7 copy.23
  184.9 0.0 copy-done.1
  184.9 0.7 copy.24
Async XLA Ops:
  177.1 2.6 %copy-start = (bf16[22528,128]{1,0:T(8,128)(2,1)S(1)}, bf16[22528,128]{1,0:T(8,128)(2,1)}, u32[]{:S(2)}) copy-start(bf16[22528,128]{1,0:T(8,128)(2,1)} %get-tuple-element.15.full) | copy-start | bytes 17301508
  179.8 4.5 %copy-start.2 = (bf16[16,6272]{1,0:T(8,128)(2,1)S(1)}, bf16[16,6272]{1,0:T(8,128)(2,1)}, u32[]{:S(2)}) copy-start(bf16[16,6272]{1,0:T(8,128)(2,1)} %get-tuple-element.13) | copy-start | bytes 602116
  179.8 5.2 %copy-start.1 = (bf16[16,6272]{1,0:T(8,128)(2,1)S(1)}, bf16[16,6272]{1,0:T(8,128)(2,1)}, u32[]{:S(2)}) copy-start(bf16[16,6272]{1,0:T(8,128)(2,1)} %get-tuple-element.14) | copy-start | bytes 602116

commit v2 on v1

--- a/solution.py
+++ b/solution.py
@@ -41,15 +41,15 @@
     return total.reshape(CH, 128)
 
 
-def prepare(src, tgt, cnt, wig, rad, w0, w1, w2, wg, w0t, w1t, w2t, wgt, wf, radt, ohs, oht):
+def prepare(src, tgt, cnt, wig, rad, wf, radt, ohs, oht):
     edges = src.shape[1]
 
-    def spread_row(k, _):
+    def spread_row(j, _):
         for q in range(4):
-            wf[q, k, 0:49, :] = wig[k, :, q * 128 : (q + 1) * 128].astype(F32)
+            wf[q, j, 0:29, :] = wig[j, :, q * 128 : (q + 1) * 128].astype(F32)
         return 0
 
-    lax.fori_loop(0, 29, spread_row, 0)
+    lax.fori_loop(0, 49, spread_row, 0)
     node = lax.broadcasted_iota(jnp.int32, (128, edges), 0)
     slot = lax.broadcasted_iota(jnp.int32, (128, edges), 1)
     ohs[...] = jnp.where(node == src[...], 1.0, 0.0).astype(BF)
@@ -57,19 +57,14 @@
     oht[...] = jnp.where((node == tgt[...]) & live, 1.0, 0.0).astype(BF)
     radt[...] = rad[...].astype(F32).T
 
-    def turn(block, out, size):
-        def step(i, _):
-            at = pl.multiple_of(i * 128, 128)
-            out[:, pl.ds(at, 128)] = block[pl.ds(at, 128), :].T
-            return 0
-
-        lax.fori_loop(0, size // 128, step, 0)
-
-    turn(w0, w0t, 896)
-    for i in range(2):
-        turn(w1.at[i], w1t.at[i], 768)
-        turn(w2.at[i], w2t.at[i], 640)
-    wgt[...] = wg[...].T
+
+def turn(block, out):
+    def step(i, _):
+        at = pl.multiple_of(i * 128, 128)
+        out[:, pl.ds(at, 128)] = block[pl.ds(at, 128), :].T
+        return 0
+
+    lax.fori_loop(0, block.shape[0] // 128, step, 0)
 
 
 INTERPRET = False
@@ -77,8 +72,8 @@
 
 def row(wf, q, k, j):
     if INTERPRET:
-        return jnp.broadcast_to(wf[q, k, pl.ds(j, 1), :], (8, 128))
-    return wf[q, k, pl.ds(j, 8, stride=0), :]
+        return jnp.broadcast_to(wf[q, j, pl.ds(k, 1), :], (8, 128))
+    return wf[q, j, pl.ds(k, 8, stride=0), :]
 
 
 def tiles(body):
@@ -130,7 +125,7 @@
     return slice(l * l * 128, (l + 1) * (l + 1) * 128)
 
 
-def forward(nodes, wf, radt, ohs, w0t, w1t, w2t, wgt, gbuf, R, mix, gate):
+def forward(nodes, wf, radt, ohs, w0t, w1t, w2t, wgt, gbuf, R, mix, gate, hook):
     for l in range(7):
         gbuf[0 : (2 * l + 1) * 128, :] = tn(nodes[:, cols(l)], ohs[...]).astype(BF)
 
@@ -138,6 +133,7 @@
             R[pl.ds(k * 128 + c0, CH), pl.ds(e0, 128)] = (v * radt[pl.ds(c0, CH), pl.ds(e0, 128)]).astype(BF)
 
         turn_in(l, wf, gbuf, emit)
+        hook(l)
 
     def zero(e):
         mix[0:896, e] = nn(w0t[...], R[0:896, e])
@@ -154,7 +150,7 @@
         halves(pair)
 
 
-def send_messages(wf, mix, gate, oht, bk, agg):
+def send_messages(wf, mix, gate, oht, bk, agg, hook):
     for l in range(7):
         def load(k, c0, e0):
             v = mix[pl.ds(k * 128 + c0, CH), pl.ds(e0, 128)]
@@ -163,6 +159,7 @@
 
         turn_out(l, wf, load, bk)
         agg[:, cols(l)] = nt(oht[...], bk[0 : (2 * l + 1) * 128, :]).astype(BF)
+        hook(l)
 
 
 def backward(cot, wf, oht, wg, gbuf, mix, gate, G, gl, direct):
@@ -225,21 +222,24 @@
         halves(pair)
 
 
-def source_grads(wf, ohs, R, bk, gn):
+def source_grads(wf, ohs, R, bk, gn, hook):
     for l in range(7):
         def load(k, c0, e0):
             return R[pl.ds(k * 128 + c0, CH), pl.ds(e0, 128)].astype(F32)
 
         turn_out(l, wf, load, bk)
         gn[:, cols(l)] = nt(ohs[...], bk[0 : (2 * l + 1) * 128, :]).astype(BF)
+        hook(l)
 
 
 HALF = TOTAL // 2
 MESH = pl.DeviceIdType.MESH
-PEERS = [(dz, dy) for dz in range(2) for dy in range(4) if (dz, dy) != (0, 0)]
-COLORS = ((0, 4096, (0, 1, 2)), (4096, 4096, (1, 2, 0)), (8192, 3072, (2, 0, 1)))
+CUT = 20 * 128
+FIRST, REST = slice(0, CUT), slice(CUT, 6272)
+COLORS = ((0, 3072, (0, 1, 2)), (3072, 3072, (0, 2, 1)), (6144, 3072, (1, 2, 0)), (9216, 2048, (2, 0, 1)))
+N = len(COLORS)
 SLOT_ROWS = sum(3 * (size // 4 + size // 16 + size // 64) for _, size, _ in COLORS)
-N_SEMS = 4 * 7 + 2 + 2 * 27
+N_SEMS = 2 * 14 + 2 * 11 + 2 * N + 2 * 9 * N
 
 
 class Links:
@@ -258,15 +258,11 @@
         pos[axis] = (pos[axis] + step) % 4
         return self.at(*pos, self.core)
 
-    def graph_peer(self, dz, dy):
-        return (self.dp, ((self.g // 4 + dz) % 2) * 4 + (self.g % 4 + dy) % 4)
-
     def other_core(self):
         return self.at(*self.pos, 1 - self.core)
 
     def greet(self):
-        peers = [self.graph_peer(*p) for p in PEERS]
-        peers += [self.along(0, 1), self.along(0, 2), self.along(0, 3), self.along(2, 1), self.along(2, 3)]
+        peers = [self.along(axis, step) for axis in range(3) for step in (1, 2, 3)]
         peers.append(self.other_core())
         barrier = pltpu.get_barrier_semaphore()
         for peer in peers:
@@ -292,27 +288,77 @@
     return pl.ds(pl.multiple_of(i * 16, 16), n)
 
 
-def gather_start(links, x, full):
-    mine = rows16(links.g)
-    out = [links.copy(x, full.at[mine], links.graph_peer(*p)) for p in PEERS]
-    full[mine, :] = x[...]
-    return out
-
-
-def scatter_start(links, part, slots):
-    out = []
-    for i, p in enumerate(PEERS):
-        peer = links.graph_peer(*p)
-        out.append(links.copy(part.at[rows16(peer[1])], slots.at[i], peer))
-    return out
-
-
-def scatter_finish(links, copies, part, slots, out):
-    done(copies)
-    total = part[rows16(links.g), :].astype(F32)
-    for i in range(len(PEERS)):
-        total += slots[i].astype(F32)
-    out[...] = total.astype(BF)
+class Gather:
+    def __init__(self, links, x, full):
+        self.links, self.full = links, full
+        y = links.pos[1]
+        across = links.g + 4 - 8 * (links.g // 4)
+        own, self.other = rows16(links.g), rows16(across)
+        self.column = [rows16(links.g - y + (y + 4 - d) % 4) for d in (1, 3, 2)]
+        self.over = [links.copy(x.at[:, FIRST], full.at[own, FIRST], links.along(2, 2))]
+        self.side = [links.copy(x.at[:, REST], full.at[own, REST], links.along(1, d)) for d in (1, 3, 2)]
+        self.last = [links.copy(x.at[:, REST], full.at[own, REST], links.along(2, 2))]
+        self.last += [links.copy(x.at[:, FIRST], full.at[own, FIRST], links.along(1, d)) for d in (1, 3, 2)]
+        full[own, :] = x[...]
+
+    def relay_over(self):
+        done(self.over)
+        part = self.full.at[self.other, FIRST]
+        self.last += [self.links.copy(part, part, self.links.along(1, d)) for d in (1, 3, 2)]
+
+    def relay_side(self):
+        for c, rows in zip(self.side, self.column):
+            c.wait()
+            part = self.full.at[rows, REST]
+            self.last.append(self.links.copy(part, part, self.links.along(2, 2)))
+
+    def finish(self):
+        done(self.last)
+
+
+class Scatter:
+    def __init__(self, links, part, out, near, far, send_far, last_far, pile, last_near):
+        self.links, self.part, self.out = links, part, out
+        self.near, self.far, self.send_far, self.last_far = near, far, send_far, last_far
+        self.pile, self.last_near = pile, last_near
+        y = links.pos[1]
+        self.y = y
+        self.here = links.g - y
+        self.there = 4 - self.here
+        self.a, self.b = [], []
+        column = pl.ds(pl.multiple_of(self.there * 16, 16), 64)
+        self.b.append(links.copy(part.at[column, REST], pile, links.along(2, 2)))
+        for i, d in enumerate((1, 3, 2)):
+            peer = (y + d) % 4
+            for ref, base in ((far, self.there), (near, self.here)):
+                self.a.append(links.copy(part.at[rows16(base + peer), FIRST], ref.at[i], links.along(1, d)))
+
+    def middle(self):
+        links, part, y = self.links, self.part, self.y
+        done(self.a)
+        total = part[rows16(self.there + y), FIRST].astype(F32)
+        for i in range(3):
+            total += self.far[i].astype(F32)
+        self.send_far[...] = total.astype(BF)
+        self.last = [links.copy(self.send_far, self.last_far, links.along(2, 2))]
+        done(self.b)
+        for i in range(4):
+            rows = pl.ds(i * 16, 16)
+            mine = part[rows16(self.here + i), REST].astype(F32)
+            self.pile[rows, :] = (mine + self.pile[rows, :].astype(F32)).astype(BF)
+        for i, d in enumerate((1, 3, 2)):
+            self.last.append(links.copy(self.pile.at[rows16((y + d) % 4)], self.last_near.at[i], links.along(1, d)))
+
+    def finish(self):
+        done(self.last)
+        total = self.part[rows16(self.here + self.y), FIRST].astype(F32) + self.last_far[...].astype(F32)
+        for i in range(3):
+            total += self.near[i].astype(F32)
+        self.out[:, FIRST] = total.astype(BF)
+        total = self.pile[rows16(self.y), :].astype(F32)
+        for i in range(3):
+            total += self.last_near[i].astype(F32)
+        self.out[:, REST] = total.astype(BF)
 
 
 def add_rows(dst, d0, srcs, n):
@@ -332,119 +378,166 @@
         lax.fori_loop(0, n // step, body, 0)
 
 
-def swap_start(links, g, inbox):
-    away = pl.multiple_of((1 - links.core) * HALF, 16)
-    return [links.copy(g.at[pl.ds(away, HALF)], inbox, links.other_core())]
-
-
-def reduce_all(links, swap, g, inbox, slots, mid, small, full):
-    home = links.core * HALF
-    done(swap)
-    add_rows(g, home, [(g, home), (inbox, 0)], HALF)
-    waiting, src, at = {}, {}, 0
-    for c, (base, size, axes) in enumerate(COLORS):
-        src[c] = (g, home + base)
-    slot_at, place = {}, {}
-    for c, (base, size, axes) in enumerate(COLORS):
-        for s in range(3):
-            slot_at[c, s] = at
-            at += 3 * (size // 4 ** (s + 1))
-
-    def start(c, s):
-        base, size, axes = COLORS[c]
-        n, (ref, row), axis = size // 4 ** (s + 1), src[c], axes[s]
+class SumAll:
+    def __init__(self, links, g, inbox, slots, mid, small, full):
+        self.links, self.g, self.slots, self.mid, self.small, self.full = links, g, slots, mid, small, full
+        self.inbox = inbox
+        self.home = links.core * HALF
+        away = (1 - links.core) * HALF
+        self.waiting, self.src, self.place, self.slot_at, at = {}, {}, {}, {}, 0
+        for c, (base, size, axes) in enumerate(COLORS):
+            self.src[c], self.place[c] = (g, self.home + base), self.home + base
+            for s in range(3):
+                self.slot_at[c, s] = at
+                at += 3 * (size // 4 ** (s + 1))
+            rows = pl.ds(pl.multiple_of(away + base, 16), size)
+            self.waiting[c] = [links.copy(g.at[rows], inbox.at[pl.ds(base, size)], links.other_core())]
+
+    def swapped(self, c):
+        base, size, _ = COLORS[c]
+        done(self.waiting[c])
+        at = self.home + base
+        add_rows(self.g, at, [(self.g, at), (self.inbox, base)], size)
+        self.start(c, 0)
+
+    def sizes(self, c, s):
+        return COLORS[c][1] // 4 ** (s + 1), COLORS[c][2][s]
+
+    def start(self, c, s):
+        links = self.links
+        (n, axis), (ref, row) = self.sizes(c, s), self.src[c]
         out = []
         for d in (1, 3, 2):
             j = (links.pos[axis] + d) % 4
             out.append(links.copy(
                 ref.at[pl.ds(pl.multiple_of(row + j * n, 16), n)],
-                slots.at[pl.ds(slot_at[c, s] + (d - 1) * n, n)],
+                self.slots.at[pl.ds(self.slot_at[c, s] + (d - 1) * n, n)],
                 links.along(axis, d)))
-        waiting[c] = out
-
-    def reduce(c, s):
-        base, size, axes = COLORS[c]
-        n, (ref, row), axis = size // 4 ** (s + 1), src[c], axes[s]
-        own = row + links.pos[axis] * n
-        place[c] = place.get(c, home + base) + links.pos[axis] * n
-        done(waiting[c])
-        srcs = [(ref, own)] + [(slots, slot_at[c, s] + d * n) for d in range(3)]
-        if s == 0:
-            dst, d0 = mid, base // 4
-        elif s == 1:
-            dst, d0 = small, base // 16
+        self.waiting[c] = out
+
+    def reduce(self, c, s):
+        (n, axis), (ref, row) = self.sizes(c, s), self.src[c]
+        base = COLORS[c][0]
+        own = row + self.links.pos[axis] * n
+        self.place[c] = self.place[c] + self.links.pos[axis] * n
+        done(self.waiting[c])
+        srcs = [(ref, own)] + [(self.slots, self.slot_at[c, s] + d * n) for d in range(3)]
+        dst, d0 = ((self.mid, base // 4), (self.small, base // 16), (self.full, self.place[c]))[s]
+        add_rows(dst, d0, srcs, n)
+        self.src[c] = (dst, d0)
+        if s < 2:
+            self.start(c, s + 1)
         else:
-            dst, d0 = full, place[c]
-        add_rows(dst, d0, srcs, n)
-        src[c] = (dst, d0)
-
-    def share(c, s):
-        base, size, axes = COLORS[c]
-        n, axis = size // 4 ** (s + 1), axes[s]
-        rows = pl.ds(pl.multiple_of(place[c], 16), n)
-        waiting[c] = [links.copy(full.at[rows], full.at[rows], links.along(axis, d)) for d in (1, 3, 2)]
-        place[c] = place[c] - links.pos[axis] * n
-
-    for c in range(3):
-        start(c, 0)
-    for s in range(3):
-        for c in range(3):
-            reduce(c, s)
-            if s < 2:
-                start(c, s + 1)
-            else:
-                share(c, 2)
-    for s in (1, 0):
-        for c in range(3):
-            done(waiting[c])
-            share(c, s)
-    for c in range(3):
-        done(waiting[c])
-    mine = pl.ds(pl.multiple_of(home, 16), HALF)
-    done([links.copy(full.at[mine], full.at[mine], links.other_core())])
+            self.share(c, 2)
+
+    def share(self, c, s):
+        n, axis = self.sizes(c, s)
+        rows = self.full.at[pl.ds(pl.multiple_of(self.place[c], 16), n)]
+        if s < 2:
+            done(self.waiting[c])
+        self.waiting[c] = [self.links.copy(rows, rows, self.links.along(axis, d)) for d in (1, 3, 2)]
+        self.place[c] = self.place[c] - self.links.pos[axis] * n
+
+    def back(self, c):
+        done(self.waiting[c])
+        rows = self.full.at[pl.ds(pl.multiple_of(self.place[c], 16), COLORS[c][1])]
+        self.waiting[c] = [self.links.copy(rows, rows, self.links.other_core())]
+
+    def each(self, step, *args):
+        for c in range(N):
+            step(c, *args)
+
+    def finish(self):
+        for c in range(N):
+            done(self.waiting[c])
 
 
 def layer_kernel(x, cx, src, tgt, cnt, wig, rad, w0, w1, w2, wg, agg, gn, full,
                  nodes, cot, w0t, w1t, w2t, wgt, wf, radt, ohs, oht, gbuf, R, mix, G, gate, gl, direct, bk,
-                 pagg, slots1, slots2, g, inbox, slots, mid, small, send, recv):
+                 pagg, near1, far1, send1, last1, pile1, lastn1, near2, far2, send2, last2, pile2, lastn2,
+                 g, inbox, slots, mid, small, send, recv):
     links = Links(send, recv)
     links.greet()
-    arriving = gather_start(links, x, nodes)
-    prepare(src, tgt, cnt, wig, rad, w0, w1, w2, wg, w0t, w1t, w2t, wgt, wf, radt, ohs, oht)
-    done(arriving)
-    arriving = gather_start(links, cx, cot)
-    forward(nodes, wf, radt, ohs, w0t, w1t, w2t, wgt, gbuf, R, mix, gate)
-    send_messages(wf, mix, gate, oht, bk, pagg)
-    done(arriving)
-    leaving = scatter_start(links, pagg, slots1)
+    gather = Gather(links, x, nodes)
+    prepare(src, tgt, cnt, wig, rad, wf, radt, ohs, oht)
+    gather.relay_over()
+    turn(w0, w0t)
+    turn(w1.at[0], w1t.at[0])
+    gather.relay_side()
+    turn(w1.at[1], w1t.at[1])
+    for i in range(2):
+        turn(w2.at[i], w2t.at[i])
+    turn(wg, wgt)
+    gather.finish()
+    gather = Gather(links, cx, cot)
+
+    def hook(l):
+        if l == 3:
+            gather.relay_over()
+        if l == 5:
+            gather.relay_side()
+
+    forward(nodes, wf, radt, ohs, w0t, w1t, w2t, wgt, gbuf, R, mix, gate, hook)
+    gather.finish()
     low = backward(cot, wf, oht, wg, gbuf, mix, gate, G, gl, direct)
     weight_grads(R, G, mix, low, g)
-    swap = swap_start(links, g, inbox)
-    scatter_finish(links, leaving, pagg, slots1, agg)
+    total = SumAll(links, g, inbox, slots, mid, small, full)
+
+    def hook(l):
+        if l == 4:
+            total.each(total.swapped)
+
+    send_messages(wf, mix, gate, oht, bk, pagg, hook)
+    first = Scatter(links, pagg, agg, near1, far1, send1, last1, pile1, lastn1)
     rotated_grads(radt, w0, w1, w2, G, R)
-    source_grads(wf, ohs, R, bk, nodes)
-    leaving = scatter_start(links, nodes, slots2)
-    reduce_all(links, swap, g, inbox, slots, mid, small, full)
-    scatter_finish(links, leaving, nodes, slots2, gn)
-
-
-def unpack_kernel(full, zero, one, two, last, b0, b1, b2, b3, sems):
-    for p in range(7):
-        b0[:, p * 128 : (p + 1) * 128] = full[p * 896 : (p + 1) * 896, :].astype(F32)
-    copies = [pltpu.make_async_copy(b0, zero, sems.at[0])]
-    copies[0].start()
-    for buf, out, base, n, s in ((b1, one, ONE_AT, 768, 1), (b2, two, TWO_AT, 640, 3)):
-        for i in range(2):
-            for p in range(n // 128):
-                at = base + (i * (n // 128) + p) * n
-                buf[i, :, p * 128 : (p + 1) * 128] = full[at : at + n, :].astype(F32)
-            copies.append(pltpu.make_async_copy(buf.at[i], out.at[i], sems.at[s + i]))
-            copies[-1].start()
-    b3[...] = full[GATE_AT:USED, :].astype(F32)
-    copies.append(pltpu.make_async_copy(b3, last, sems.at[5]))
-    copies[-1].start()
-    for c in copies:
+
+    def hook(l):
+        if l == 4:
+            total.each(total.reduce, 0)
+            first.middle()
+        if l == 5:
+            total.each(total.reduce, 1)
+
+    source_grads(wf, ohs, R, bk, nodes, hook)
+    second = Scatter(links, nodes, gn, near2, far2, send2, last2, pile2, lastn2)
+    total.each(total.reduce, 2)
+    total.each(total.share, 1)
+    first.finish()
+    total.each(total.share, 0)
+    second.middle()
+    total.each(total.back)
+    second.finish()
+    total.finish()
+
+
+def unpack_kernel(full, agg, gn, agg_o, gn_o, zero, one, two, last, buf, b0, b1, b2, b3, s_in, s_out):
+    pieces = [(full.at[pl.ds(lo, hi - lo)], buf.at[pl.ds(lo, hi - lo)]) for lo, hi in zip(BOUNDS[:-1], BOUNDS[1:])]
+    loads = [pltpu.make_async_copy(a, b, s_in.at[i]) for i, (a, b) in enumerate(pieces)]
+    for c in loads:
+        c.start()
+    stores = [pltpu.make_async_copy(agg, agg_o, s_out.at[6]), pltpu.make_async_copy(gn, gn_o, s_out.at[7])]
+    for c in stores:
+        c.start()
+    targets = [(b0, zero), (b1.at[0], one.at[0]), (b1.at[1], one.at[1]), (b2.at[0], two.at[0]), (b2.at[1], two.at[1]), (b3, last)]
+    for i, (tile, out) in enumerate(targets):
+        loads[i].wait()
+        n = tile.shape[0]
+        for p in range(n // 128):
+            at = BOUNDS[i] + p * n
+            tile[:, p * 128 : (p + 1) * 128] = buf[at : at + n, :].astype(F32)
+        stores.append(pltpu.make_async_copy(tile, out, s_out.at[i]))
+        stores[-1].start()
+    for c in stores:
         c.wait()
+
+
+BOUNDS = (0, ONE_AT, ONE_AT + 4608, TWO_AT, TWO_AT + 3200, GATE_AT, USED)
+
+
+def scatter_scratch():
+    first, rest = CUT, 6272 - CUT
+    shapes = ((3, 16, first), (3, 16, first), (16, first), (16, first), (64, rest), (3, 16, rest))
+    return [pltpu.VMEM(shape, BF) for shape in shapes]
 
 
 def per_device(nodes, sources, targets, counts, wigner, radial, cotangent, w0, w1, w2, wg):
@@ -467,7 +560,7 @@
             pltpu.VMEM((2, 768, 768), BF),
             pltpu.VMEM((2, 640, 640), BF),
             pltpu.VMEM((128, 128), BF),
-            pltpu.VMEM((4, 29, 56, 128), F32),
+            pltpu.VMEM((4, 49, 32, 128), F32),
             pltpu.VMEM((128, 512), F32),
             pltpu.VMEM((128, 512), BF),
             pltpu.VMEM((128, 512), BF),
@@ -480,8 +573,8 @@
             pltpu.VMEM((128, 512), F32),
             pltpu.VMEM((13 * 128, 512), BF),
             pltpu.VMEM((128, 6272), BF),
-            pltpu.VMEM((7, 16, 6272), BF),
-            pltpu.VMEM((7, 16, 6272), BF),
+            *scatter_scratch(),
+            *scatter_scratch(),
             pltpu.VMEM((TOTAL, 128), BF),
             pltpu.VMEM((HALF, 128), BF),
             pltpu.VMEM((SLOT_ROWS, 128), BF),
@@ -494,27 +587,22 @@
             vmem_limit_bytes=67043328, collective_id=0, has_side_effects=True
         ),
         name="edge_layer",
-    )(nodes[0], cotangent[0], sources, targets, counts, wigner[0], radial[0], w0, w1, w2, wg)
-    zero, one, two, last = pl.pallas_call(
+    )(nodes[0], cotangent[0], sources, targets, counts, jnp.swapaxes(wigner[0], 0, 1), radial[0], w0, w1, w2, wg)
+    return_shapes = [(16, 6272)] * 2 + [(896, 896), (2, 768, 768), (2, 640, 640), (128, 128)]
+    agg, gn, zero, one, two, last = pl.pallas_call(
         unpack_kernel,
-        out_shape=(
-            jax.ShapeDtypeStruct((896, 896), F32),
-            jax.ShapeDtypeStruct((2, 768, 768), F32),
-            jax.ShapeDtypeStruct((2, 640, 640), F32),
-            jax.ShapeDtypeStruct((128, 128), F32),
-        ),
-        in_specs=[vm],
-        out_specs=(hbm,) * 4,
+        out_shape=[jax.ShapeDtypeStruct(shape, BF if i < 2 else F32) for i, shape in enumerate(return_shapes)],
+        in_specs=[hbm, vm, vm],
+        out_specs=[hbm] * 6,
         scratch_shapes=[
-            pltpu.VMEM((896, 896), F32),
-            pltpu.VMEM((2, 768, 768), F32),
-            pltpu.VMEM((2, 640, 640), F32),
-            pltpu.VMEM((128, 128), F32),
+            pltpu.VMEM((USED, 128), BF),
+            *[pltpu.VMEM(shape, F32) for shape in return_shapes[2:]],
             dma((6,)),
+            dma((8,)),
         ],
-        compiler_params=pltpu.CompilerParams(vmem_limit_bytes=40 << 20),
+        compiler_params=pltpu.CompilerParams(vmem_limit_bytes=67043328),
         name="unpack",
-    )(full)
+    )(full, agg, gn)
     return agg[None], gn[None], zero, one, two, last
 
 

time: 186 us -> 141 us (0.76)
  Pallas kernels: 177 us -> 139 us
  local copies, waits for them, and re-layouts: 7.42 us -> 0 us
    pallas_call x1, Pallas kernels: 172 us -> 132 us  [per_device(): pl.pallas_call(layer_kernel, out_shape=(jax.ShapeDtypeStruct((16, 6272),...]
    unnamed x9 -> x0, local copies, waits for them, and re-layouts: 7.42 us -> none
    pallas_call x1, Pallas kernels: 4.46 us -> 7.12 us  [per_device(): pl.pallas_call(unpack_kernel, out_shape=[jax.ShapeDtypeStruct(shape, BF i...]
where the time goes in v2:
time: 141 us
  Pallas kernels  139 us (99%)
  between operations  1.47 us (1%)
    pallas_call x1, Pallas kernels, per_device(): pl.pallas_call(layer_kernel, out_shape=(jax.ShapeDtypeStruct((16, 6272),...  132 us
    pallas_call x1, Pallas kernels, per_device(): pl.pallas_call(unpack_kernel, out_shape=[jax.ShapeDtypeStruct(shape, BF i...  7.12 us

profile of v2, /device:TPU:1, one launch (start us, length us, event | category | flops | bytes accessed | tf_op | source)
XLA Modules:
  0.0 140.9 jit_solution(4631861447672995569)
XLA Ops:
  1.3 132.4 %edge_layer.1 = (bf16[16,6272]{1,0:T(8,128)(2,1)}, bf16[16,6272]{1,0:T(8,128)(2,1)}, bf16[22528,128]{1,0:T(8,128)(2,1)}) custom-call(bf16[16,6272]{1,0:T(8,128)(2,1)} %bitcast.9, bf16[16,6272]{1,0:T(8,128)(2,1)} %bitcast.10, s32[1,512]{1,0:T(1,128)} %src.1, s32[1,512]{1,0:T(1,128)} %tgt.1, s32[1,1]{1,0:T(1,128)S(6)} %copy.17.cnt, ...), custom_call_target="tpu_custom_call" | custom-call | tf_op jit(solution)/shard_map/edge_layer/pallas_call | solution.py:547
  133.6 7.1 %unpack.1 = (bf16[16,6272]{1,0:T(8,128)(2,1)}, bf16[16,6272]{1,0:T(8,128)(2,1)}, f32[896,896]{1,0:T(8,128)}, f32[2,768,768]{2,1,0:T(8,128)}, f32[2,640,640]{2,1,0:T(8,128)}, /*index=5*/f32[128,128]{1,0:T(8,128)}) custom-call(bf16[22528,128]{1,0:T(8,128)(2,1)} %get-tuple-element.15.full, bf16[16,6272]{1,0:T(8,128)(2,1)} %get-tuple-element.16.agg, ...), custom_call_target="tpu_custom_call" | custom-call | tf_op jit(solution)/shard_map/unpack/pallas_call | solution.py:592

commit v3 on v2

--- a/solution.py
+++ b/solution.py
@@ -234,12 +234,21 @@
 
 HALF = TOTAL // 2
 MESH = pl.DeviceIdType.MESH
-CUT = 20 * 128
+CUT = 24 * 128
 FIRST, REST = slice(0, CUT), slice(CUT, 6272)
-COLORS = ((0, 3072, (0, 1, 2)), (3072, 3072, (0, 2, 1)), (6144, 3072, (1, 2, 0)), (9216, 2048, (2, 0, 1)))
+COLORS = (
+    (0, 2048, (0, 1, 2)),
+    (2048, 2048, (1, 2, 0)),
+    (4096, 2048, (2, 0, 1)),
+    (6144, 2048, (0, 2, 1)),
+    (8192, 2048, (1, 0, 2)),
+    (10240, 1024, (2, 1, 0)),
+)
+EARLY, LATE, ALL = (0, 1, 2), (3, 4, 5), (0, 1, 2, 3, 4, 5)
 N = len(COLORS)
 SLOT_ROWS = sum(3 * (size // 4 + size // 16 + size // 64) for _, size, _ in COLORS)
-N_SEMS = 2 * 14 + 2 * 11 + 2 * N + 2 * 9 * N
+N_SEMS = 2 * 14 + 2 * 11 + 5 * N + 2 * 9 * N
+N_SEND = 56
 
 
 class Links:
@@ -249,6 +258,7 @@
         self.pos = (dp // 4, self.g % 4, (self.g // 4) * 2 + (dp // 2) % 2)
         self.core = dp % 2
         self.send, self.recv, self.used = send, recv, 0
+        self.free = list(range(N_SEND - 1, -1, -1))
 
     def at(self, x, y, z, core):
         return ((x * 2 + z % 2) * 2 + core, (z // 2) * 4 + y)
@@ -270,13 +280,23 @@
         pl.semaphore_wait(barrier, len(peers))
 
     def copy(self, src, dst, peer):
+        slot = self.free.pop()
         out = pltpu.make_async_remote_copy(
-            src_ref=src, dst_ref=dst, send_sem=self.send.at[self.used], recv_sem=self.recv.at[self.used],
+            src_ref=src, dst_ref=dst, send_sem=self.send.at[slot], recv_sem=self.recv.at[self.used],
             device_id=peer, device_id_type=MESH,
         )
         self.used += 1
         out.start()
-        return out
+        return Sent(self, out, slot)
+
+
+class Sent:
+    def __init__(self, links, out, slot):
+        self.links, self.out, self.slot = links, out, slot
+
+    def wait(self):
+        self.out.wait()
+        self.links.free.append(self.slot)
 
 
 def done(copies):
@@ -381,7 +401,7 @@
 class SumAll:
     def __init__(self, links, g, inbox, slots, mid, small, full):
         self.links, self.g, self.slots, self.mid, self.small, self.full = links, g, slots, mid, small, full
-        self.inbox = inbox
+        self.inbox, self.swaps = inbox, []
         self.home = links.core * HALF
         away = (1 - links.core) * HALF
         self.waiting, self.src, self.place, self.slot_at, at = {}, {}, {}, {}, 0
@@ -398,7 +418,6 @@
         done(self.waiting[c])
         at = self.home + base
         add_rows(self.g, at, [(self.g, at), (self.inbox, base)], size)
-        self.start(c, 0)
 
     def sizes(self, c, s):
         return COLORS[c][1] // 4 ** (s + 1), COLORS[c][2][s]
@@ -436,20 +455,24 @@
         if s < 2:
             done(self.waiting[c])
         self.waiting[c] = [self.links.copy(rows, rows, self.links.along(axis, d)) for d in (1, 3, 2)]
+        if s == 0:
+            self.swaps.append(self.links.copy(rows, rows, self.links.other_core()))
         self.place[c] = self.place[c] - self.links.pos[axis] * n
 
     def back(self, c):
-        done(self.waiting[c])
-        rows = self.full.at[pl.ds(pl.multiple_of(self.place[c], 16), COLORS[c][1])]
-        self.waiting[c] = [self.links.copy(rows, rows, self.links.other_core())]
-
-    def each(self, step, *args):
-        for c in range(N):
+        n, axis = self.sizes(c, 0)
+        for copy, d in zip(self.waiting[c], (1, 3, 2)):
+            copy.wait()
+            block = (self.links.pos[axis] + 4 - d) % 4
+            rows = self.full.at[pl.ds(pl.multiple_of(self.place[c] + block * n, 16), n)]
+            self.swaps.append(self.links.copy(rows, rows, self.links.other_core()))
+
+    def finish(self):
+        done(self.swaps)
+
+    def each(self, colors, step, *args):
+        for c in colors:
             step(c, *args)
-
-    def finish(self):
-        for c in range(N):
-            done(self.waiting[c])
 
 
 def layer_kernel(x, cx, src, tgt, cnt, wig, rad, w0, w1, w2, wg, agg, gn, full,
@@ -484,28 +507,31 @@
     total = SumAll(links, g, inbox, slots, mid, small, full)
 
     def hook(l):
-        if l == 4:
-            total.each(total.swapped)
+        colors = {3: EARLY, 5: LATE}.get(l, ())
+        total.each(colors, total.swapped)
+        total.each(colors, total.start, 0)
 
     send_messages(wf, mix, gate, oht, bk, pagg, hook)
     first = Scatter(links, pagg, agg, near1, far1, send1, last1, pile1, lastn1)
     rotated_grads(radt, w0, w1, w2, G, R)
 
     def hook(l):
+        if l == 2:
+            total.each(EARLY, total.reduce, 0)
         if l == 4:
-            total.each(total.reduce, 0)
+            total.each(LATE, total.reduce, 0)
             first.middle()
         if l == 5:
-            total.each(total.reduce, 1)
+            total.each(ALL, total.reduce, 1)
 
     source_grads(wf, ohs, R, bk, nodes, hook)
     second = Scatter(links, nodes, gn, near2, far2, send2, last2, pile2, lastn2)
-    total.each(total.reduce, 2)
-    total.each(total.share, 1)
+    total.each(ALL, total.reduce, 2)
+    total.each(ALL, total.share, 1)
     first.finish()
-    total.each(total.share, 0)
+    total.each(ALL, total.share, 0)
     second.middle()
-    total.each(total.back)
+    total.each(ALL, total.back)
     second.finish()
     total.finish()
 
@@ -580,7 +606,7 @@
             pltpu.VMEM((SLOT_ROWS, 128), BF),
             pltpu.VMEM((HALF // 4, 128), BF),
             pltpu.VMEM((HALF // 16, 128), BF),
-            dma((N_SEMS,)),
+            dma((N_SEND,)),
             dma((N_SEMS,)),
         ],
         compiler_params=pltpu.CompilerParams(

time: 141 us -> 134 us (0.950)
  Pallas kernels: 139 us -> 133 us
    pallas_call x1, Pallas kernels: 132 us -> 126 us  [per_device(): pl.pallas_call(layer_kernel, out_shape=(jax.ShapeDtypeStruct((16, 6272),...]
where the time goes in v3:
time: 134 us
  Pallas kernels  133 us (99%)
  between operations  1.47 us (1%)
    pallas_call x1, Pallas kernels, per_device(): pl.pallas_call(layer_kernel, out_shape=(jax.ShapeDtypeStruct((16, 6272),...  126 us
    pallas_call x1, Pallas kernels, per_device(): pl.pallas_call(unpack_kernel, out_shape=[jax.ShapeDtypeStruct(shape, BF i...  7.12 us

profile of v3, /device:TPU:1, one launch (start us, length us, event | category | flops | bytes accessed | tf_op | source)
XLA Modules:
  0.0 134.2 jit_solution(17203824537588743970)
XLA Ops:
  1.3 125.6 %edge_layer.1 = (bf16[16,6272]{1,0:T(8,128)(2,1)}, bf16[16,6272]{1,0:T(8,128)(2,1)}, bf16[22528,128]{1,0:T(8,128)(2,1)}) custom-call(bf16[16,6272]{1,0:T(8,128)(2,1)} %bitcast.9, bf16[16,6272]{1,0:T(8,128)(2,1)} %bitcast.10, s32[1,512]{1,0:T(1,128)} %src.1, s32[1,512]{1,0:T(1,128)} %tgt.1, s32[1,1]{1,0:T(1,128)S(6)} %copy.17.cnt, ...), custom_call_target="tpu_custom_call" | custom-call | tf_op jit(solution)/shard_map/edge_layer/pallas_call | solution.py:573
  126.9 7.1 %unpack.1 = (bf16[16,6272]{1,0:T(8,128)(2,1)}, bf16[16,6272]{1,0:T(8,128)(2,1)}, f32[896,896]{1,0:T(8,128)}, f32[2,768,768]{2,1,0:T(8,128)}, f32[2,640,640]{2,1,0:T(8,128)}, /*index=5*/f32[128,128]{1,0:T(8,128)}) custom-call(bf16[22528,128]{1,0:T(8,128)(2,1)} %get-tuple-element.15.full, bf16[16,6272]{1,0:T(8,128)(2,1)} %get-tuple-element.16.agg, ...), custom_call_target="tpu_custom_call" | custom-call | tf_op jit(solution)/shard_map/unpack/pallas_call | solution.py:618

commit v4 on v3

--- a/solution.py
+++ b/solution.py
@@ -586,7 +586,7 @@
             pltpu.VMEM((2, 768, 768), BF),
             pltpu.VMEM((2, 640, 640), BF),
             pltpu.VMEM((128, 128), BF),
-            pltpu.VMEM((4, 49, 32, 128), F32),
+            pltpu.VMEM((4, 49, 40, 128), F32),
             pltpu.VMEM((128, 512), F32),
             pltpu.VMEM((128, 512), BF),
             pltpu.VMEM((128, 512), BF),

time: 134 us -> 134 us (level)
  no operation moved by 1% of the time
where the time goes in v4:
time: 134 us
  Pallas kernels  133 us (99%)
  between operations  1.47 us (1%)
    pallas_call x1, Pallas kernels, per_device(): pl.pallas_call(layer_kernel, out_shape=(jax.ShapeDtypeStruct((16, 6272),...  126 us
    pallas_call x1, Pallas kernels, per_device(): pl.pallas_call(unpack_kernel, out_shape=[jax.ShapeDtypeStruct(shape, BF i...  7.12 us

profile of v4, /device:TPU:1, one launch (start us, length us, event | category | flops | bytes accessed | tf_op | source)
XLA Modules:
  0.0 134.2 jit_solution(2611145834670864644)
XLA Ops:
  1.3 125.6 %edge_layer.1 = (bf16[16,6272]{1,0:T(8,128)(2,1)}, bf16[16,6272]{1,0:T(8,128)(2,1)}, bf16[22528,128]{1,0:T(8,128)(2,1)}) custom-call(bf16[16,6272]{1,0:T(8,128)(2,1)} %bitcast.9, bf16[16,6272]{1,0:T(8,128)(2,1)} %bitcast.10, s32[1,512]{1,0:T(1,128)} %src.1, s32[1,512]{1,0:T(1,128)} %tgt.1, s32[1,1]{1,0:T(1,128)S(6)} %copy.17.cnt, ...), custom_call_target="tpu_custom_call" | custom-call | tf_op jit(solution)/shard_map/edge_layer/pallas_call | solution.py:573
  126.9 7.1 %unpack.1 = (bf16[16,6272]{1,0:T(8,128)(2,1)}, bf16[16,6272]{1,0:T(8,128)(2,1)}, f32[896,896]{1,0:T(8,128)}, f32[2,768,768]{2,1,0:T(8,128)}, f32[2,640,640]{2,1,0:T(8,128)}, /*index=5*/f32[128,128]{1,0:T(8,128)}) custom-call(bf16[22528,128]{1,0:T(8,128)(2,1)} %get-tuple-element.15.full, bf16[16,6272]{1,0:T(8,128)(2,1)} %get-tuple-element.16.agg, ...), custom_call_target="tpu_custom_call" | custom-call | tf_op jit(solution)/shard_map/unpack/pallas_call | solution.py:618
